TPU v7x, 32 devices: a whole 2x2x4 slice. The times are simulated.
32 devices in a mesh: blk: 8 (over z, x), col: 4 (over y, core).
Axes of the slice: x: 2, y: 2, z: 4, core: 2. Of those that a mesh axis runs over, the one named last changes fastest.
Arguments:
- points: bfloat16 [4096, 128], P(('blk', 'col')), may hold values from -4.5 to 4.5
- targets: float32 [4096, 32], P(('blk', 'col')), may hold values from -6 to 6
- pivots: int32 [2, 256], replicated, may hold values from 0 to 4095, as said below
Outputs:
- factor: bfloat16 [4096, 512], P(('blk', 'col'))
- solution: float32 [4096, 32], P(('blk', 'col'))
- residual: float32 [4096, 32], P(('blk', 'col'))
Inputs may be any that keep to these rules, and one draw needn't show every extreme that they name: `pivots`: the 512 indices are distinct; 0 and 4095 are among them.
All inputs are finite; a program needn't handle non-finite values.
Results may differ from a plain program's by a relative error of at most 0.012.
Values may be sent and summed in bfloat16 or wider, within the bound.
A program may use at most 64 MiB of HBM per device.

v0:
```python
import jax
import jax.numpy as jnp
from jax import lax
from jax.sharding import PartitionSpec as P

FEATURES = 128
ITERS = 3
noise_level = 0.5
jitter_level = 0.05
highest = lax.Precision.HIGHEST


def squared_norms(point_rows):
    wide_rows = point_rows.astype(jnp.float32)
    return jnp.sum(wide_rows * wide_rows, axis=1)


def kernel_block(left_rows, left_norms, right_rows, right_norms):
    inner = lax.dot_general(
        left_rows, right_rows, (((1,), (1,)), ((), ())), preferred_element_type=jnp.float32
    )
    distance = left_norms[:, None] + right_norms[None, :] - 2.0 * inner
    return jnp.exp(-2.0 * distance / FEATURES)


def lower_solve(lower_factor, right_rows):
    return jax.scipy.linalg.solve_triangular(lower_factor, right_rows.T, lower=True).T


def build_factor(point_rows, first_pick, second_pick):
    row_norms = squared_norms(point_rows)
    first_norms = squared_norms(first_pick)
    second_norms = squared_norms(second_pick)
    identity_piv = jnp.eye(first_pick.shape[0], dtype=jnp.float32)
    first_chol = jnp.linalg.cholesky(
        kernel_block(first_pick, first_norms, first_pick, first_norms) + jitter_level * identity_piv
    )
    first_coef = lower_solve(
        first_chol, kernel_block(point_rows, row_norms, first_pick, first_norms)
    )
    shared_coef = lower_solve(
        first_chol, kernel_block(second_pick, second_norms, first_pick, first_norms)
    )
    schur_block = (
        kernel_block(second_pick, second_norms, second_pick, second_norms)
        + jitter_level * identity_piv
        - jnp.dot(shared_coef, shared_coef.T, precision=highest)
    )
    second_chol = jnp.linalg.cholesky(schur_block)
    second_cross = kernel_block(point_rows, row_norms, second_pick, second_norms) - jnp.dot(
        first_coef, shared_coef.T, precision=highest
    )
    second_coef = lower_solve(second_chol, second_cross)
    return jnp.concatenate([first_coef, second_coef], axis=1)


def per_device(points, targets, pivots):
    row_count = points.shape[0]
    piv_count = pivots.shape[1]
    shard_index = lax.axis_index("blk") * lax.axis_size("col") + lax.axis_index("col")
    first_row = shard_index * row_count
    flat_pivots = pivots.reshape(-1)
    owned = (
        flat_pivots[:, None] == first_row + jnp.arange(row_count, dtype=jnp.int32)[None, :]
    ).astype(jnp.float32)
    local_pick = jnp.dot(owned, points.astype(jnp.float32), precision=highest)
    picked = lax.psum(local_pick, ("blk", "col")).astype(jnp.bfloat16)
    wide_factor = build_factor(points, picked[:piv_count], picked[piv_count:])
    factor = wide_factor.astype(jnp.bfloat16)
    local_gram = lax.dot_general(
        wide_factor, wide_factor, (((0,), (0,)), ((), ())), precision=highest
    )
    gram = lax.psum(local_gram, ("blk", "col"))
    gram = gram + noise_level * jnp.eye(2 * piv_count, dtype=jnp.float32)
    gram_chol = jnp.linalg.cholesky(gram)

    def precondition(residual_now):
        local_proj = lax.dot_general(
            wide_factor, residual_now, (((0,), (0,)), ((), ())), precision=highest
        )
        square_sum, projection = lax.psum(
            (jnp.sum(residual_now * residual_now, axis=0), local_proj), ("blk", "col")
        )
        coefficients = jax.scipy.linalg.cho_solve((gram_chol, True), projection)
        scaled = (
            residual_now - jnp.dot(wide_factor, coefficients, precision=highest)
        ) / noise_level
        return (scaled, (square_sum - jnp.sum(projection * coefficients, axis=0)) / noise_level)

    own_block = lax.all_gather(points, "col", axis=0, tiled=True)
    own_norms = squared_norms(own_block)

    def tile_add(total, key_rows, key_norms, direction_rows):
        weights = kernel_block(own_block, own_norms, key_rows, key_norms)
        return total + jnp.dot(weights, direction_rows, precision=highest)

    solution = jnp.zeros_like(targets)
    residual = targets
    direction_now, inner_now = precondition(residual)
    for step_index in range(ITERS):
        empty = jnp.zeros((own_block.shape[0], direction_now.shape[1]), jnp.float32)
        add_key_rows = lax.all_gather(points.astype(jnp.float32), "blk", axis=0, tiled=True).astype(
            jnp.bfloat16
        )
        fold_direction_rows = lax.all_gather(direction_now, "blk", axis=0, tiled=True)
        piece_rows = add_key_rows.shape[0]
        splits = piece_rows // row_count

        def scan_step(carry, operands):
            return (tile_add(carry, operands[0], operands[1], operands[2]), None)

        stacked = (
            add_key_rows.reshape(splits, row_count, add_key_rows.shape[1]),
            squared_norms(add_key_rows).reshape(splits, row_count),
            fold_direction_rows.reshape(splits, row_count, fold_direction_rows.shape[1]),
        )
        result, unused = lax.scan(scan_step, empty, stacked)
        image = (
            lax.psum_scatter(result, "col", scatter_dimension=0, tiled=True)
            + noise_level * direction_now
        )
        curvature = lax.psum(jnp.sum(direction_now * image, axis=0), ("blk", "col"))
        step_size = inner_now / curvature
        solution = solution + step_size * direction_now
        residual = residual - step_size * image
        if step_index + 1 < ITERS:
            scaled, inner_next = precondition(residual)
            direction_now = scaled + inner_next / inner_now * direction_now
            inner_now = inner_next
    return (factor, solution, residual)


def solution(mesh):
    return jax.shard_map(
        per_device,
        mesh=mesh,
        in_specs=(P(("blk", "col"), None), P(("blk", "col"), None), P()),
        out_specs=(P(("blk", "col"), None), P(("blk", "col"), None), P(("blk", "col"), None)),
        check_vma=False,
    )
```

profile of v0, /device:TPU:0, one launch (start us, length us, event | category | flops | bytes accessed | tf_op | source)
XLA Modules:
  0.0 1023.6 jit_solution(6104249524737897158)
XLA Ops:
  8.9 44.6 %all-reduce.14 = bf16[512,128]{1,0:T(8,128)(2,1)S(1)} all-reduce(f32[512,128]{1,0:T(8,128)S(1)} %fusion.59), channel_id=1, replica_groups=mesh['blk'=8,'col'=4] {'blk','col'}, use_global_device_ids=true, to_apply=%region_0.0 | all-reduce | flops 65536 | bytes 393216 | tf_op jit(solution)/shard_map/psum | solution.py:67
  54.1 11.7 %cholesky.354 = f32[128,128]{1,0:T(8,128)S(1)} custom-call(f32[128,128]{1,0:T(8,128)S(1)} %cholesky.404), custom_call_target="Cholesky" | custom-call | tf_op jit(solution)/shard_map/jit(cholesky)/cholesky | solution.py:35
  65.9 9.8 custom-call.54
  76.4 11.7 %cholesky.364 = f32[128,128]{1,0:T(8,128)S(1)} custom-call(f32[128,128]{1,0:T(8,128)S(1)} %convolution_subtract_fusion.8), custom_call_target="Cholesky" | custom-call | tf_op jit(solution)/shard_map/jit(cholesky)/cholesky | solution.py:35
  91.9 4.4 while.53
  92.7 1.4 dynamic-slice.27
  94.8 1.4 dynamic-slice.27
  96.3 19.7 %custom-call.55 = f32[2,128,128]{1,2,0:T(8,128)S(1)} custom-call(f32[2,128,128]{2,1,0:T(8,128)S(1)} %get-tuple-element.391), custom_call_target="InvertDiagBlocksLowerTriangular" | custom-call | tf_op jit(solution)/shard_map/jit(_solve_triangular)/triangular_solve | solution.py:27
  118.7 11.7 %cholesky.381 = f32[128,128]{1,0:T(8,128)S(1)} custom-call(f32[128,128]{1,0:T(8,128)S(1)} %cholesky.407), custom_call_target="Cholesky" | custom-call | tf_op jit(solution)/shard_map/jit(cholesky)/cholesky | solution.py:49
  130.5 9.8 custom-call.56
  140.8 11.7 %cholesky.391 = f32[128,128]{1,0:T(8,128)S(1)} custom-call(f32[128,128]{1,0:T(8,128)S(1)} %convolution_subtract_fusion.6), custom_call_target="Cholesky" | custom-call | tf_op jit(solution)/shard_map/jit(cholesky)/cholesky | solution.py:49
  155.6 4.0 while.54
  156.2 1.4 bitcast_dynamic-update-slice_fusion.7
  158.2 1.4 bitcast_dynamic-update-slice_fusion.7
  159.6 19.7 %custom-call.57 = f32[2,128,128]{1,2,0:T(8,128)S(1)} custom-call(f32[2,128,128]{2,1,0:T(8,128)S(1)} %get-tuple-element.392), custom_call_target="InvertDiagBlocksLowerTriangular" | custom-call | tf_op jit(solution)/shard_map/jit(_solve_triangular)/triangular_solve | solution.py:27
  180.7 2.0 fusion.225
  183.8 5.4 all_gather.17
  189.2 31.2 %all_gather.18 = bf16[1024,128]{1,0:T(8,128)(2,1)S(1)} all-gather(bf16[128,128]{1,0:T(8,128)(2,1)S(1)} %copy-done.6), channel_id=1, replica_groups=mesh['blk'=8,'col'=4] {'blk'}, dimensions={0}, use_global_device_ids=true | all-gather | bytes 294912 | tf_op jit(solution)/shard_map/all_gather | solution.py:102
  221.3 93.0 %all-reduce.13.cloned.1.call-done = (f32[512,512]{1,0:T(8,128)}, f32[512,32]{0,1:T(8,128)}) async-done(((f32[512,512]{1,0:T(8,128)}, f32[512,32]{0,1:T(8,128)}), (f32[512,512]{1,0:T(8,128)}, f32[512,32]{0,1:T(8,128)})) %all-reduce.13.cloned.1.call-update) | async-done | bytes 1114128 | tf_op jit(solution)/shard_map/psum | solution.py:73
  317.1 11.7 %cholesky.166 = f32[128,128]{1,0:T(8,128)S(1)} custom-call(f32[128,128]{1,0:T(8,128)S(1)} %cholesky.410), custom_call_target="Cholesky" | custom-call | tf_op jit(solution)/shard_map/jit(cholesky)/cholesky | solution.py:75
  329.0 9.8 custom-call.42
  339.5 11.7 %cholesky.189 = f32[128,128]{1,0:T(8,128)S(1)} custom-call(f32[128,128]{1,0:T(8,128)S(1)} %cholesky.414), custom_call_target="Cholesky" | custom-call | tf_op jit(solution)/shard_map/jit(cholesky)/cholesky | solution.py:75
  352.5 9.9 custom-call.43
  363.1 11.7 %cholesky.292 = f32[128,128]{1,0:T(8,128)S(1)} custom-call(f32[128,128]{1,0:T(8,128)S(1)} %cholesky.419), custom_call_target="Cholesky" | custom-call | tf_op jit(solution)/shard_map/jit(cholesky)/cholesky | solution.py:75
  375.6 9.8 custom-call.58
  386.0 11.9 %cholesky.305 = f32[128,128]{1,0:T(8,128)S(1)} custom-call(f32[128,128]{1,0:T(8,128)S(1)} %convolution_subtract_fusion.9), custom_call_target="Cholesky" | custom-call | tf_op jit(solution)/shard_map/jit(cholesky)/cholesky | solution.py:75
  401.3 10.4 %while.55 = (s32[]{:T(128)}, f32[512,512]{1,0:T(8,128)S(1)}, s32[4,2]{0,1:T(2,128)S(1)}, f32[4,128,128]{2,1,0:T(8,128)}, s32[]{:T(128)}) while((s32[]{:T(128)}, f32[512,512]{1,0:T(8,128)S(1)}, s32[4,2]{0,1:T(2,128)S(1)}, f32[4,128,128]{2,1,0:T(8,128)}, s32[]{:T(128)}) %tuple.173), condition=%wide.while_cond.1, body=%wide.while_body.1.sunk | while | flops 2 | bytes 132705 | solution.py:84
  401.9 2.0 bitcast_dynamic-update-slice_fusion.8
  404.5 2.0 bitcast_dynamic-update-slice_fusion.8
  407.1 2.0 bitcast_dynamic-update-slice_fusion.8
  409.7 2.0 bitcast_dynamic-update-slice_fusion.8
  411.7 40.1 %custom-call.59 = f32[4,128,128]{1,2,0:T(8,128)S(1)} custom-call(f32[4,128,128]{2,1,0:T(8,128)} %get-tuple-element.393), custom_call_target="InvertDiagBlocksLowerTriangular" | custom-call | tf_op jit(solution)/shard_map/jit(_cho_solve)/triangular_solve | solution.py:84
  455.8 30.6 %all_gather.19 = f32[1024,32]{0,1:T(8,128)S(1)} all-gather(f32[128,32]{0,1:T(8,128)S(1)} %get-tuple-element.538), channel_id=1, replica_groups=mesh['blk'=8,'col'=4] {'blk'}, dimensions={0}, use_global_device_ids=true | all-gather | bytes 147456 | tf_op jit(solution)/shard_map/all_gather | solution.py:105
  487.2 11.4 %while.50 = (s32[]{:T(128)}, f32[512,32]{0,1:T(8,128)S(1)}, f32[512]{0:T(512)S(1)}, f32[8,128]{1,0:T(8,128)S(1)}, bf16[8,128,128]{2,1,0:T(8,128)(2,1)}, /*index=...) while((s32[]{:T(128)}, f32[512,32]{0,1:T(8,128)S(1)}, ...), condition=%wide.region_24.29_spmd.clone, body=%wide.region_23.28_spmd.clone.sunk | while | flops 42237952 | bytes 888943 | solution.py:117
  499.5 19.3 %reduce-scatter.4.cloned.1.call-done = f32[128,32]{0,1:T(8,128)} async-done(((f32[512,32]{0,1:T(8,128)}), f32[128,32]{0,1:T(8,128)}) %reduce-scatter.4.cloned.1.call-update) | async-done | bytes 16400 | tf_op jit(solution)/shard_map/reduce_scatter | solution.py:119
  519.6 39.3 %all-reduce.2 = (f32[32]{0:T(128)S(1)}, f32[32]{0:T(128)S(1)}) all-reduce(f32[32]{0:T(128)S(1)} %get-tuple-element.506, f32[32]{0:T(128)S(1)} %multiply_reduce_fusion.13), channel_id=1, replica_groups=mesh['blk'=8,'col'=4] {'blk','col'}, use_global_device_ids=true, to_apply=%region_27.32 | all-reduce | flops 64 | bytes 512 | tf_op jit(solution)/shard_map/psum | solution.py:122
  560.2 41.0 %psum.82 = f32[32]{0:T(128)S(1)} all-reduce(f32[32]{0:T(128)S(1)} %get-tuple-element.504), channel_id=1, replica_groups=mesh['blk'=8,'col'=4] {'blk','col'}, use_global_device_ids=true, to_apply=%region_29.34 | all-reduce | flops 32 | bytes 256 | tf_op jit(solution)/shard_map/psum | solution.py:81
  601.2 79.3 %all-reduce.9.cloned.1.call-done = f32[512,32]{0,1:T(8,128)} async-done(((f32[512,32]{0,1:T(8,128)}), f32[512,32]{0,1:T(8,128)}) %all-reduce.9.cloned.1.call-update) | async-done | bytes 65552 | tf_op jit(solution)/shard_map/psum | solution.py:81
  684.9 30.5 %all_gather.20 = f32[1024,32]{0,1:T(8,128)S(1)} all-gather(f32[128,32]{0,1:T(8,128)S(1)} %fusion.53), channel_id=1, replica_groups=mesh['blk'=8,'col'=4] {'blk'}, dimensions={0}, use_global_device_ids=true | all-gather | bytes 147456 | tf_op jit(solution)/shard_map/all_gather | solution.py:105
  715.6 11.4 %while.51 = (s32[]{:T(128)}, f32[512,32]{0,1:T(8,128)S(1)}, f32[512]{0:T(512)S(1)}, f32[8,128]{1,0:T(8,128)S(1)}, bf16[8,128,128]{2,1,0:T(8,128)(2,1)}, /*index=...) while((s32[]{:T(128)}, f32[512,32]{0,1:T(8,128)S(1)}, ...), condition=%wide.region_33.38_spmd.clone, body=%wide.region_32.37_spmd.clone.sunk | while | flops 42237952 | bytes 888943 | solution.py:117
  727.7 19.1 %reduce-scatter.6.cloned.1.call-done = f32[128,32]{0,1:T(8,128)} async-done(((f32[512,32]{0,1:T(8,128)}), f32[128,32]{0,1:T(8,128)}) %reduce-scatter.6.cloned.1.call-update) | async-done | bytes 16400 | tf_op jit(solution)/shard_map/reduce_scatter | solution.py:119
  747.7 39.3 %psum.84 = f32[32]{0:T(128)S(1)} all-reduce(f32[32]{0:T(128)S(1)} %multiply_reduce_fusion.10), channel_id=1, replica_groups=mesh['blk'=8,'col'=4] {'blk','col'}, use_global_device_ids=true, to_apply=%region_36.41 | all-reduce | flops 32 | bytes 256 | tf_op jit(solution)/shard_map/psum | solution.py:122
  788.3 41.2 %psum.85 = f32[32]{0:T(128)S(1)} all-reduce(f32[32]{0:T(128)S(1)} %get-tuple-element.502), channel_id=1, replica_groups=mesh['blk'=8,'col'=4] {'blk','col'}, use_global_device_ids=true, to_apply=%region_38.43 | all-reduce | flops 32 | bytes 256 | tf_op jit(solution)/shard_map/psum | solution.py:81
  829.5 79.0 %all-reduce.11.cloned.1.call-done = f32[512,32]{0,1:T(8,128)} async-done(((f32[512,32]{0,1:T(8,128)}), f32[512,32]{0,1:T(8,128)}) %all-reduce.11.cloned.1.call-update) | async-done | bytes 65552 | tf_op jit(solution)/shard_map/psum | solution.py:81
  912.9 30.5 %all_gather.21 = f32[1024,32]{0,1:T(8,128)S(1)} all-gather(f32[128,32]{0,1:T(8,128)S(1)} %fusion.54), channel_id=1, replica_groups=mesh['blk'=8,'col'=4] {'blk'}, dimensions={0}, use_global_device_ids=true | all-gather | bytes 147456 | tf_op jit(solution)/shard_map/all_gather | solution.py:105
  943.6 11.4 %while.52 = (s32[]{:T(128)}, f32[512,32]{0,1:T(8,128)S(1)}, f32[512]{0:T(512)S(1)}, f32[8,128]{1,0:T(8,128)S(1)}, bf16[8,128,128]{2,1,0:T(8,128)(2,1)}, /*index=...) while((s32[]{:T(128)}, f32[512,32]{0,1:T(8,128)S(1)}, ...), condition=%wide.region_42.47_spmd.clone, body=%wide.region_41.46_spmd.clone.sunk | while | flops 42237952 | bytes 888943 | solution.py:117
  955.7 19.1 %reduce-scatter.8.cloned.1.call-done = f32[128,32]{0,1:T(8,128)} async-done(((f32[512,32]{0,1:T(8,128)}), f32[128,32]{0,1:T(8,128)}) %reduce-scatter.8.cloned.1.call-update) | async-done | bytes 16400 | tf_op jit(solution)/shard_map/reduce_scatter | solution.py:119
  976.4 39.2 %psum.87 = f32[32]{0:T(128)S(1)} all-reduce(f32[32]{0:T(128)S(1)} %multiply_reduce_fusion.8), channel_id=1, replica_groups=mesh['blk'=8,'col'=4] {'blk','col'}, use_global_device_ids=true, to_apply=%region_45.50 | all-reduce | flops 32 | bytes 256 | tf_op jit(solution)/shard_map/psum | solution.py:122
  (283 shorter events, 81.9 us)
Async XLA Ops:
  7.2 307.2 %all-reduce.13.cloned.1.call-start = ((), (), s32[]{:S(2)}) async-start(), calls=%async_computation.8 | async-start | bytes 2228224 | tf_op jit(solution)/shard_map/psum | solution.py:73
  7.2 0.7 copy-start.14
  88.1 0.8 copy-start.6
  180.7 2.0 copy-start.10
  183.7 335.1 %reduce-scatter.4.cloned.1.call-start = ((), (), s32[]{:S(2)}) async-start(), calls=%async_computation.3 | async-start | bytes 81920 | tf_op jit(solution)/shard_map/reduce_scatter | solution.py:119
  220.4 0.7 copy-start.1
  315.7 1.2 copy-start
  401.3 50.6 %copy-start.7 = (f32[512,32]{0,1:T(8,128)S(1)}, f32[512,32]{0,1:T(8,128)}, u32[]{:S(2)}) copy-start(f32[512,32]{0,1:T(8,128)} %get-tuple-element.499) | copy-start | bytes 196612
  454.8 0.7 copy-start.11
  486.4 0.8 copy-start.2
  498.6 0.6 copy-start.3
  499.2 181.2 %all-reduce.9.cloned.1.call-start = ((), (), s32[]{:S(2)}) async-start(), calls=%async_computation.4 | async-start | bytes 131072 | tf_op jit(solution)/shard_map/psum | solution.py:81
  560.2 186.6 %reduce-scatter.6.cloned.1.call-start = ((), (), s32[]{:S(2)}) async-start(), calls=%async_computation.5 | async-start | bytes 81920 | tf_op jit(solution)/shard_map/reduce_scatter | solution.py:119
  680.5 1.0 copy-start.9
  727.0 0.6 copy-start.5
  727.7 180.8 %all-reduce.11.cloned.1.call-start = ((), (), s32[]{:S(2)}) async-start(), calls=%async_computation.6 | async-start | bytes 131072 | tf_op jit(solution)/shard_map/psum | solution.py:81
  746.8 40.2 %copy-start.13 = (f32[128,32]{0,1:T(8,128)S(1)}, f32[128,32]{0,1:T(8,128)}, u32[]{:S(2)}) copy-start(f32[128,32]{0,1:T(8,128)} %reduce-scatter.6.cloned.1.call-done) | copy-start | bytes 49156
  788.2 186.6 %reduce-scatter.8.cloned.1.call-start = ((), (), s32[]{:S(2)}) async-start(), calls=%async_computation.7 | async-start | bytes 81920 | tf_op jit(solution)/shard_map/reduce_scatter | solution.py:119
  908.5 1.0 copy-start.8
  955.0 0.6 copy-start.4
  975.6 40.0 %copy-start.12 = (f32[128,32]{0,1:T(8,128)S(1)}, f32[128,32]{0,1:T(8,128)}, u32[]{:S(2)}) copy-start(f32[128,32]{0,1:T(8,128)} %reduce-scatter.8.cloned.1.call-done) | copy-start | bytes 49156
Sparse Core Ops, SparseCore 0:
  183.8 130.4 all-reduce.12
  499.3 19.4 reduce-scatter.3
  560.3 120.1 all-reduce.8
  727.8 18.9 reduce-scatter.5
  788.3 120.0 all-reduce.10
  955.8 18.9 reduce-scatter.7
where the time goes:
time: 1040 us; the launch traced here: 1020 us
  blocking collectives  373 us (36%)
  waiting for transfers between devices  309 us (30%)
  other arithmetic  234 us (22%)
  matrix products  58.3 us (6%)
  local copies, waits for them, and re-layouts  26.9 us (3%)
  between operations  20.8 us (2%)
    psum x2, waiting for transfers between devices, precondition(): lax.psum((jnp.sum(residual_now * residual_now, axis=0), local_proj), ('bl...  158 us
    psum x3, blocking collectives, per_device(): curvature = lax.psum(jnp.sum(direction_now * image, axis=0), ('blk', 'col'))  118 us
    psum x1, waiting for transfers between devices, per_device(): gram = lax.psum(local_gram, ('blk', 'col'))  93 us
    all_gather x3, blocking collectives, per_device(): lax.all_gather(direction_now, 'blk', axis=0, tiled=True)  91.6 us
    psum x2, blocking collectives, precondition(): lax.psum((jnp.sum(residual_now * residual_now, axis=0), local_proj), ('bl...  82.2 us
    another operation x15, other arithmetic, per_device(): gram_chol = jnp.linalg.cholesky(gram)  79.4 us
    reduce_scatter x3, waiting for transfers between devices, per_device(): lax.psum_scatter(result, 'col', scatter_dimension=0, tiled=True)  57.5 us
    psum x1, blocking collectives, per_device(): picked = lax.psum(local_pick, ('blk', 'col')).astype(jnp.bfloat16)  44.6 us
  transfers between devices with their start and end apart: 6, of which 6 were waited for; matrix products, arithmetic and copies ran while one was open for 0% of the time, Pallas kernels for 0%

commit v1 on v0

--- a/solution.py
+++ b/solution.py
@@ -8,6 +8,11 @@
 noise_level = 0.5
 jitter_level = 0.05
 highest = lax.Precision.HIGHEST
+
+
+def axis_by_axis(value, inner_axis, outer_axis):
+    half = lax.psum(value, inner_axis)
+    return lax.psum(half, outer_axis)
 
 
 def squared_norms(point_rows):
@@ -78,8 +83,8 @@
         local_proj = lax.dot_general(
             wide_factor, residual_now, (((0,), (0,)), ((), ())), precision=highest
         )
-        square_sum, projection = lax.psum(
-            (jnp.sum(residual_now * residual_now, axis=0), local_proj), ("blk", "col")
+        square_sum, projection = axis_by_axis(
+            (jnp.sum(residual_now * residual_now, axis=0), local_proj), "blk", "col"
         )
         coefficients = jax.scipy.linalg.cho_solve((gram_chol, True), projection)
         scaled = (

time: 1040 us -> 1080 us (1.038)
  waiting for transfers between devices: 309 us -> 359 us
    psum x1, waiting for transfers between devices: 93 us -> 136 us  [per_device(): gram = lax.psum(local_gram, ('blk', 'col'))]
    psum x2 -> x6, waiting for transfers between devices: 158 us -> 184 us  [the longest x3 169 us: axis_by_axis(): half = lax.psum(value, inner_axis)]
    reduce_scatter x3, waiting for transfers between devices: 57.5 us -> 39.1 us  [per_device(): lax.psum_scatter(result, 'col', scatter_dimension=0, tiled=True)]
    psum x2 -> x6, blocking collectives: 82.2 us -> 78.5 us  [the longest x3 61.1 us: axis_by_axis(): half = lax.psum(value, inner_axis)]
  transfers between devices with their start and end apart: 6 -> 10, of which waited for: 6 -> 8; matrix products, arithmetic and copies ran while one was open for 0% -> 13% of each run, Pallas kernels for 0% -> 0%
where the time goes in v1:
time: 1080 us; the launch traced here: 1070 us
  blocking collectives  367 us (34%)
  waiting for transfers between devices  359 us (33%)
  other arithmetic  234 us (22%)
  matrix products  59.1 us (5%)
  local copies, waits for them, and re-layouts  27.6 us (3%)
  between operations  21.1 us (2%)
    psum x3, waiting for transfers between devices, axis_by_axis(): half = lax.psum(value, inner_axis)  169 us
    psum x1, waiting for transfers between devices, per_device(): gram = lax.psum(local_gram, ('blk', 'col'))  136 us
    psum x3, blocking collectives, per_device(): curvature = lax.psum(jnp.sum(direction_now * image, axis=0), ('blk', 'col'))  115 us
    all_gather x3, blocking collectives, per_device(): lax.all_gather(direction_now, 'blk', axis=0, tiled=True)  91.8 us
    another operation x15, other arithmetic, per_device(): gram_chol = jnp.linalg.cholesky(gram)  79.2 us
    psum x3, blocking collectives, axis_by_axis(): half = lax.psum(value, inner_axis)  61.1 us
    psum x1, blocking collectives, per_device(): picked = lax.psum(local_pick, ('blk', 'col')).astype(jnp.bfloat16)  44.6 us
    another operation x4, other arithmetic, precondition(): coefficients = jax.scipy.linalg.cho_solve((gram_chol, True), projection)  40.3 us
  transfers between devices with their start and end apart: 10, of which 8 were waited for; matrix products, arithmetic and copies ran while one was open for 13% of the time, Pallas kernels for 0%

profile of v1, /device:TPU:0, one launch (start us, length us, event | category | flops | bytes accessed | tf_op | source)
XLA Modules:
  0.0 1069.5 jit_solution(4703764759442106833)
XLA Ops:
  8.9 44.6 %all-reduce.24 = bf16[512,128]{1,0:T(8,128)(2,1)S(1)} all-reduce(f32[512,128]{1,0:T(8,128)S(1)} %fusion.59), channel_id=1, replica_groups=mesh['blk'=8,'col'=4] {'blk','col'}, use_global_device_ids=true, to_apply=%region_0.0 | all-reduce | flops 65536 | bytes 393216 | tf_op jit(solution)/shard_map/psum | solution.py:72
  54.1 11.7 %cholesky.354 = f32[128,128]{1,0:T(8,128)S(1)} custom-call(f32[128,128]{1,0:T(8,128)S(1)} %cholesky.404), custom_call_target="Cholesky" | custom-call | tf_op jit(solution)/shard_map/jit(cholesky)/cholesky | solution.py:40
  65.9 9.8 custom-call.54
  76.4 11.7 %cholesky.364 = f32[128,128]{1,0:T(8,128)S(1)} custom-call(f32[128,128]{1,0:T(8,128)S(1)} %convolution_subtract_fusion.8), custom_call_target="Cholesky" | custom-call | tf_op jit(solution)/shard_map/jit(cholesky)/cholesky | solution.py:40
  91.9 4.4 while.53
  96.3 19.7 %custom-call.55 = f32[2,128,128]{1,2,0:T(8,128)S(1)} custom-call(f32[2,128,128]{2,1,0:T(8,128)S(1)} %get-tuple-element.391), custom_call_target="InvertDiagBlocksLowerTriangular" | custom-call | tf_op jit(solution)/shard_map/jit(_solve_triangular)/triangular_solve | solution.py:32
  118.7 11.7 %cholesky.381 = f32[128,128]{1,0:T(8,128)S(1)} custom-call(f32[128,128]{1,0:T(8,128)S(1)} %cholesky.407), custom_call_target="Cholesky" | custom-call | tf_op jit(solution)/shard_map/jit(cholesky)/cholesky | solution.py:54
  130.5 9.8 custom-call.56
  140.8 11.7 %cholesky.391 = f32[128,128]{1,0:T(8,128)S(1)} custom-call(f32[128,128]{1,0:T(8,128)S(1)} %convolution_subtract_fusion.6), custom_call_target="Cholesky" | custom-call | tf_op jit(solution)/shard_map/jit(cholesky)/cholesky | solution.py:54
  155.5 4.0 while.54
  159.6 19.7 %custom-call.57 = f32[2,128,128]{1,2,0:T(8,128)S(1)} custom-call(f32[2,128,128]{2,1,0:T(8,128)S(1)} %get-tuple-element.392), custom_call_target="InvertDiagBlocksLowerTriangular" | custom-call | tf_op jit(solution)/shard_map/jit(_solve_triangular)/triangular_solve | solution.py:32
  182.4 2.0 fusion.225
  184.5 5.4 all_gather.17
  190.0 30.7 %all_gather.18 = bf16[1024,128]{1,0:T(8,128)(2,1)S(1)} all-gather(bf16[128,128]{1,0:T(8,128)(2,1)S(1)} %copy-done.6), channel_id=1, replica_groups=mesh['blk'=8,'col'=4] {'blk'}, dimensions={0}, use_global_device_ids=true | all-gather | bytes 294912 | tf_op jit(solution)/shard_map/all_gather | solution.py:107
  221.6 29.2 %all-reduce.13.cloned.1.call-done = f32[512,32]{0,1:T(8,128)} async-done(((f32[512,32]{0,1:T(8,128)}), f32[512,32]{0,1:T(8,128)}) %all-reduce.13.cloned.1.call-update) | async-done | bytes 65552 | tf_op jit(solution)/shard_map/psum | solution.py:14
  251.0 135.9 %all-reduce.11.cloned.1.call-done = f32[512,512]{1,0:T(8,128)} async-done(((f32[512,512]{1,0:T(8,128)}), f32[512,512]{1,0:T(8,128)}) %all-reduce.11.cloned.1.call-update) | async-done | bytes 1048592 | tf_op jit(solution)/shard_map/psum | solution.py:78
  389.7 11.7 %cholesky.166 = f32[128,128]{1,0:T(8,128)S(1)} custom-call(f32[128,128]{1,0:T(8,128)S(1)} %cholesky.410), custom_call_target="Cholesky" | custom-call | tf_op jit(solution)/shard_map/jit(cholesky)/cholesky | solution.py:80
  401.6 9.8 custom-call.42
  412.1 11.7 %cholesky.189 = f32[128,128]{1,0:T(8,128)S(1)} custom-call(f32[128,128]{1,0:T(8,128)S(1)} %cholesky.414), custom_call_target="Cholesky" | custom-call | tf_op jit(solution)/shard_map/jit(cholesky)/cholesky | solution.py:80
  425.1 10.0 custom-call.43
  435.7 11.7 %cholesky.292 = f32[128,128]{1,0:T(8,128)S(1)} custom-call(f32[128,128]{1,0:T(8,128)S(1)} %cholesky.419), custom_call_target="Cholesky" | custom-call | tf_op jit(solution)/shard_map/jit(cholesky)/cholesky | solution.py:80
  448.2 9.8 custom-call.58
  458.6 11.7 %cholesky.305 = f32[128,128]{1,0:T(8,128)S(1)} custom-call(f32[128,128]{1,0:T(8,128)S(1)} %convolution_subtract_fusion.9), custom_call_target="Cholesky" | custom-call | tf_op jit(solution)/shard_map/jit(cholesky)/cholesky | solution.py:80
  473.9 10.4 while.55
  477.1 2.0 bitcast_dynamic-update-slice_fusion.8
  482.3 2.0 bitcast_dynamic-update-slice_fusion.8
  484.3 40.1 %custom-call.59 = f32[4,128,128]{1,2,0:T(8,128)S(1)} custom-call(f32[4,128,128]{2,1,0:T(8,128)} %get-tuple-element.393), custom_call_target="InvertDiagBlocksLowerTriangular" | custom-call | tf_op jit(solution)/shard_map/jit(_cho_solve)/triangular_solve | solution.py:89
  529.2 30.5 %all_gather.19 = f32[1024,32]{0,1:T(8,128)S(1)} all-gather(f32[128,32]{0,1:T(8,128)S(1)} %get-tuple-element.534), channel_id=1, replica_groups=mesh['blk'=8,'col'=4] {'blk'}, dimensions={0}, use_global_device_ids=true | all-gather | bytes 147456 | tf_op jit(solution)/shard_map/all_gather | solution.py:110
  560.6 11.4 %while.50 = (s32[]{:T(128)}, f32[512,32]{0,1:T(8,128)S(1)}, f32[512]{0:T(512)S(1)}, f32[8,128]{1,0:T(8,128)S(1)}, bf16[8,128,128]{2,1,0:T(8,128)(2,1)}, /*index=...) while((s32[]{:T(128)}, f32[512,32]{0,1:T(8,128)S(1)}, ...), condition=%wide.region_26.31_spmd.clone, body=%wide.region_25.30_spmd.clone.sunk | while | flops 42237952 | bytes 888943 | solution.py:122
  572.7 20.4 %psum.123 = f32[32]{0:T(128)S(1)} all-reduce(f32[32]{0:T(128)S(1)} %multiply_reduce_fusion.13), channel_id=1, replica_groups=mesh['blk'=8,'col'=4] {'blk'}, use_global_device_ids=true, to_apply=%region_20.25 | all-reduce | flops 32 | bytes 256 | tf_op jit(solution)/shard_map/psum | solution.py:14
  593.1 5.8 psum.124
  599.9 36.9 %psum.125 = f32[32]{0:T(128)S(1)} all-reduce(f32[32]{0:T(128)S(1)} %get-tuple-element.502), channel_id=1, replica_groups=mesh['blk'=8,'col'=4] {'blk','col'}, use_global_device_ids=true, to_apply=%region_29.34 | all-reduce | flops 32 | bytes 256 | tf_op jit(solution)/shard_map/psum | solution.py:127
  638.1 69.8 %all-reduce.17.cloned.1.call-done = f32[512,32]{0,1:T(8,128)} async-done(((f32[512,32]{0,1:T(8,128)}), f32[512,32]{0,1:T(8,128)}) %all-reduce.17.cloned.1.call-update) | async-done | bytes 65552 | tf_op jit(solution)/shard_map/psum | solution.py:14
  707.9 20.4 %psum.126 = f32[32]{0:T(128)S(1)} all-reduce(f32[32]{0:T(128)S(1)} %get-tuple-element.500), channel_id=1, replica_groups=mesh['blk'=8,'col'=4] {'blk'}, use_global_device_ids=true, to_apply=%region_31.36 | all-reduce | flops 32 | bytes 256 | tf_op jit(solution)/shard_map/psum | solution.py:14
  728.3 5.6 psum.127
  733.9 7.6 all-reduce.19.cloned.1.call-done
  745.9 30.7 %all_gather.20 = f32[1024,32]{0,1:T(8,128)S(1)} all-gather(f32[128,32]{0,1:T(8,128)S(1)} %fusion.53), channel_id=1, replica_groups=mesh['blk'=8,'col'=4] {'blk'}, dimensions={0}, use_global_device_ids=true | all-gather | bytes 147456 | tf_op jit(solution)/shard_map/all_gather | solution.py:110
  776.8 11.4 %while.51 = (s32[]{:T(128)}, f32[512,32]{0,1:T(8,128)S(1)}, f32[512]{0:T(512)S(1)}, f32[8,128]{1,0:T(8,128)S(1)}, bf16[8,128,128]{2,1,0:T(8,128)(2,1)}, /*index=...) while((s32[]{:T(128)}, f32[512,32]{0,1:T(8,128)S(1)}, ...), condition=%wide.region_37.42_spmd.clone, body=%wide.region_36.41_spmd.clone.sunk | while | flops 42237952 | bytes 888943 | solution.py:122
  788.9 19.5 %reduce-scatter.6.cloned.1.call-done = f32[128,32]{0,1:T(8,128)} async-done(((f32[512,32]{0,1:T(8,128)}), f32[128,32]{0,1:T(8,128)}) %reduce-scatter.6.cloned.1.call-update) | async-done | bytes 16400 | tf_op jit(solution)/shard_map/reduce_scatter | solution.py:124
  809.3 39.3 %psum.130 = f32[32]{0:T(128)S(1)} all-reduce(f32[32]{0:T(128)S(1)} %multiply_reduce_fusion.10), channel_id=1, replica_groups=mesh['blk'=8,'col'=4] {'blk','col'}, use_global_device_ids=true, to_apply=%region_40.45 | all-reduce | flops 32 | bytes 256 | tf_op jit(solution)/shard_map/psum | solution.py:127
  849.9 70.1 %all-reduce.21.cloned.1.call-done = f32[512,32]{0,1:T(8,128)} async-done(((f32[512,32]{0,1:T(8,128)}), f32[512,32]{0,1:T(8,128)}) %all-reduce.21.cloned.1.call-update) | async-done | bytes 65552 | tf_op jit(solution)/shard_map/psum | solution.py:14
  920.0 20.4 %psum.131 = f32[32]{0:T(128)S(1)} all-reduce(f32[32]{0:T(128)S(1)} %get-tuple-element.498), channel_id=1, replica_groups=mesh['blk'=8,'col'=4] {'blk'}, use_global_device_ids=true, to_apply=%region_42.47 | all-reduce | flops 32 | bytes 256 | tf_op jit(solution)/shard_map/psum | solution.py:14
  940.4 5.9 psum.132
  946.3 7.5 all-reduce.23.cloned.1.call-done
  958.2 30.7 %all_gather.21 = f32[1024,32]{0,1:T(8,128)S(1)} all-gather(f32[128,32]{0,1:T(8,128)S(1)} %fusion.54), channel_id=1, replica_groups=mesh['blk'=8,'col'=4] {'blk'}, dimensions={0}, use_global_device_ids=true | all-gather | bytes 147456 | tf_op jit(solution)/shard_map/all_gather | solution.py:110
  989.1 11.4 %while.52 = (s32[]{:T(128)}, f32[512,32]{0,1:T(8,128)S(1)}, f32[512]{0:T(512)S(1)}, f32[8,128]{1,0:T(8,128)S(1)}, bf16[8,128,128]{2,1,0:T(8,128)(2,1)}, /*index=...) while((s32[]{:T(128)}, f32[512,32]{0,1:T(8,128)S(1)}, ...), condition=%wide.region_48.53_spmd.clone, body=%wide.region_47.52_spmd.clone.sunk | while | flops 42237952 | bytes 888943 | solution.py:122
  1001.1 19.6 %reduce-scatter.8.cloned.1.call-done = f32[128,32]{0,1:T(8,128)} async-done(((f32[512,32]{0,1:T(8,128)}), f32[128,32]{0,1:T(8,128)}) %reduce-scatter.8.cloned.1.call-update) | async-done | bytes 16400 | tf_op jit(solution)/shard_map/reduce_scatter | solution.py:124
  1022.3 39.2 %psum.135 = f32[32]{0:T(128)S(1)} all-reduce(f32[32]{0:T(128)S(1)} %multiply_reduce_fusion.8), channel_id=1, replica_groups=mesh['blk'=8,'col'=4] {'blk','col'}, use_global_device_ids=true, to_apply=%region_51.56 | all-reduce | flops 32 | bytes 256 | tf_op jit(solution)/shard_map/psum | solution.py:127
  (299 shorter events, 93.1 us)
Async XLA Ops:
  7.2 243.7 %all-reduce.13.cloned.1.call-start = ((), (), s32[]{:S(2)}) async-start(), calls=%async_computation.4 | async-start | bytes 131072 | tf_op jit(solution)/shard_map/psum | solution.py:14
  7.2 0.7 copy-start.14
  88.1 0.8 copy-start.6
  180.6 0.7 copy-start.10
  182.4 204.5 %all-reduce.11.cloned.1.call-start = ((), (), s32[]{:S(2)}) async-start(), calls=%async_computation.3 | async-start | bytes 2097152 | tf_op jit(solution)/shard_map/psum | solution.py:78
  184.5 339.9 %all-reduce.15.cloned.1.call-start = ((), (), s32[]{:S(2)}) async-start(), calls=%async_computation.5 | async-start | bytes 131072 | tf_op jit(solution)/shard_map/psum | solution.py:15
  220.7 0.7 copy-start.1
  250.9 348.2 %reduce-scatter.4.cloned.1.call-start = ((), (), s32[]{:S(2)}) async-start(), calls=%async_computation.6 | async-start | bytes 81920 | tf_op jit(solution)/shard_map/reduce_scatter | solution.py:124
  388.2 1.2 copy-start
  524.4 1.0 copy-start.7
  528.2 0.7 copy-start.11
  559.7 0.8 copy-start.2
  571.9 0.6 copy-start.3
  572.6 135.2 %all-reduce.17.cloned.1.call-start = ((), (), s32[]{:S(2)}) async-start(), calls=%async_computation.7 | async-start | bytes 131072 | tf_op jit(solution)/shard_map/psum | solution.py:14
  638.0 103.5 %all-reduce.19.cloned.1.call-start = ((), (), s32[]{:S(2)}) async-start(), calls=%async_computation.8 | async-start | bytes 131072 | tf_op jit(solution)/shard_map/psum | solution.py:15
  707.8 100.5 %reduce-scatter.6.cloned.1.call-start = ((), (), s32[]{:S(2)}) async-start(), calls=%async_computation.9 | async-start | bytes 81920 | tf_op jit(solution)/shard_map/reduce_scatter | solution.py:124
  741.5 1.0 copy-start.9
  788.2 0.6 copy-start.5
  788.8 131.2 %all-reduce.21.cloned.1.call-start = ((), (), s32[]{:S(2)}) async-start(), calls=%async_computation.10 | async-start | bytes 131072 | tf_op jit(solution)/shard_map/psum | solution.py:14
  808.4 40.2 %copy-start.13 = (f32[128,32]{0,1:T(8,128)S(1)}, f32[128,32]{0,1:T(8,128)}, u32[]{:S(2)}) copy-start(f32[128,32]{0,1:T(8,128)} %reduce-scatter.6.cloned.1.call-done) | copy-start | bytes 49156
  849.8 104.0 %all-reduce.23.cloned.1.call-start = ((), (), s32[]{:S(2)}) async-start(), calls=%async_computation.11 | async-start | bytes 131072 | tf_op jit(solution)/shard_map/psum | solution.py:15
  920.0 100.7 %reduce-scatter.8.cloned.1.call-start = ((), (), s32[]{:S(2)}) async-start(), calls=%async_computation.12 | async-start | bytes 81920 | tf_op jit(solution)/shard_map/reduce_scatter | solution.py:124
  953.8 1.0 copy-start.8
  1000.5 0.6 copy-start.4
  1021.5 40.0 %copy-start.12 = (f32[128,32]{0,1:T(8,128)S(1)}, f32[128,32]{0,1:T(8,128)}, u32[]{:S(2)}) copy-start(f32[128,32]{0,1:T(8,128)} %reduce-scatter.8.cloned.1.call-done) | copy-start | bytes 49156
Sparse Core Ops, SparseCore 0:
  182.5 68.3 all-reduce.12
  256.1 130.7 all-reduce.10
  389.2 30.7 all-reduce.14
  572.7 18.5 reduce-scatter.3
  638.1 69.6 all-reduce.16
  710.0 31.4 all-reduce.18
  788.9 19.3 reduce-scatter.5
  849.9 69.9 all-reduce.20
  922.3 31.4 all-reduce.22
  1001.2 19.4 reduce-scatter.7
